TPU v7x, 256 devices: a whole 4x4x8 slice. The times are simulated.
256 devices in a mesh: fsdp: 16 (over y, x), tensor: 16 (over z, core).
Axes of the slice: x: 4, y: 4, z: 8, core: 2. Of those that a mesh axis runs over, the one named last changes fastest.
Arguments:
- inputs: bfloat16 [3072, 8192], P('fsdp'), may hold values from -6 to 6
- cotangent: bfloat16 [3072, 8192], P('fsdp'), may hold values from -1.1953125 to 1.1953125
- up_tiles: bfloat16 [16, 64, 128, 128], P('tensor', 'fsdp'), may hold values from -0.25 to 0.25
- up_rows: int32 [16, 64], P('tensor', 'fsdp'), may hold values from 0 to 63, as said below
- up_cols: int32 [16, 64], P('tensor', 'fsdp'), may hold values from 0 to 15, as said below
- down_tiles: bfloat16 [16, 64, 128, 128], P('tensor', 'fsdp'), may hold values from -0.25 to 0.25
- down_rows: int32 [16, 64], P('tensor', 'fsdp'), may hold values from 0 to 15, as said below
- down_cols: int32 [16, 64], P('tensor', 'fsdp'), may hold values from 0 to 63, as said below
Outputs:
- input_grad: bfloat16 [3072, 8192], P('fsdp', 'tensor')
- up_grad: bfloat16 [16, 64, 128, 128], P('tensor', 'fsdp')
- down_grad: bfloat16 [16, 64, 128, 128], P('tensor', 'fsdp')
Inputs may be any that keep to these rules, and one draw needn't show every extreme that they name: `up_rows`: together with up_cols, the positions of a group's 64 tiles are distinct; slot s is held by fsdp index s // 4. `up_cols`: see up_rows. `down_rows`: together with down_cols, the positions of a group's 64 tiles are distinct; slot s is held by fsdp index s // 4. `down_cols`: see down_rows.
All inputs are finite; a program needn't handle non-finite values.
Results may differ from a plain program's by a relative error of at most 0.015.
Values may be sent and summed in bfloat16 or wider, within the bound.
A program may use at most 128 MiB of HBM per device.

v0:
```python
import jax
import jax.numpy as jnp
from jax import lax
from jax.sharding import PartitionSpec as P

FF = 32768
TILE = 128


def gelu_parts(pre):
    coef = 0.7978845608028654
    inner = coef * (pre + 0.044715 * pre * pre * pre)
    tanh_val = jnp.tanh(inner)
    act = 0.5 * pre * (1.0 + tanh_val)
    slope = 0.5 * (1.0 + tanh_val) + 0.5 * pre * (1.0 - tanh_val * tanh_val) * coef * (
        1.0 + 3.0 * 0.044715 * pre * pre
    )
    return (act, slope)


def on_device(inputs, cotangent, up_tiles, up_rows, up_cols, down_tiles, down_rows, down_cols):
    tok_count = inputs.shape[0]
    row_blocks = inputs.shape[1] // TILE
    group_cols = FF // (lax.axis_size("tensor") * TILE)
    input_blocks = inputs.reshape(tok_count, row_blocks, TILE)
    cotan_blocks = cotangent.reshape(tok_count, row_blocks, TILE)
    gathered = (
        lax.all_gather(up_tiles, "fsdp", axis=1, tiled=True),
        lax.all_gather(up_rows, "fsdp", axis=1, tiled=True),
        lax.all_gather(up_cols, "fsdp", axis=1, tiled=True),
        lax.all_gather(down_tiles, "fsdp", axis=1, tiled=True),
        lax.all_gather(down_rows, "fsdp", axis=1, tiled=True),
        lax.all_gather(down_cols, "fsdp", axis=1, tiled=True),
    )
    w_up, r_up, c_up = (gathered[0][0], gathered[1][0], gathered[2][0])
    w_down, r_down, c_down = (gathered[3][0], gathered[4][0], gathered[5][0])
    x_sel = jnp.take(input_blocks, r_up, axis=1)
    prod = jnp.einsum("tsk,skf->stf", x_sel, w_up, preferred_element_type=jnp.float32)
    pre = jax.ops.segment_sum(prod, c_up, num_segments=group_cols)
    act, slope = gelu_parts(pre)
    hidden = act.astype(jnp.bfloat16)
    dy_sel = jnp.take(cotan_blocks, c_down, axis=1)
    h_sel = jnp.take(hidden, r_down, axis=0)
    back = jnp.einsum("tsk,sfk->stf", dy_sel, w_down, preferred_element_type=jnp.float32)
    dhid = jax.ops.segment_sum(back, r_down, num_segments=group_cols)
    dpre = (dhid * slope).astype(jnp.bfloat16)
    dp_sel = jnp.take(dpre, c_up, axis=0)
    both_sum = lax.psum_scatter(
        jnp.stack(
            [
                jnp.einsum("tsk,stf->skf", x_sel, dp_sel, preferred_element_type=jnp.float32),
                jnp.einsum("stf,tsk->sfk", h_sel, dy_sel, preferred_element_type=jnp.float32),
            ],
            axis=1,
        ).astype(jnp.bfloat16),
        "fsdp",
        scatter_dimension=0,
        tiled=True,
    ).astype(jnp.float32)
    up_sum = both_sum[:, 0]
    down_sum = both_sum[:, 1]
    back_in = jnp.einsum("stf,skf->stk", dp_sel, w_up, preferred_element_type=jnp.float32)
    in_part = jax.ops.segment_sum(back_in, r_up, num_segments=row_blocks)
    own_blocks = lax.psum_scatter(
        in_part.astype(jnp.bfloat16), "tensor", scatter_dimension=0, tiled=True
    ).astype(jnp.float32)
    input_grad = jnp.transpose(own_blocks, (1, 0, 2)).reshape(tok_count, -1).astype(jnp.bfloat16)
    up_grad = up_sum.astype(jnp.bfloat16)[None]
    down_grad = down_sum.astype(jnp.bfloat16)[None]
    return (input_grad, up_grad, down_grad)


def solution(mesh):
    placed = (
        P("fsdp", None),
        P("fsdp", None),
        P("tensor", "fsdp", None, None),
        P("tensor", "fsdp"),
        P("tensor", "fsdp"),
        P("tensor", "fsdp", None, None),
        P("tensor", "fsdp"),
        P("tensor", "fsdp"),
    )
    return jax.shard_map(
        on_device,
        mesh=mesh,
        in_specs=placed,
        out_specs=(
            P("fsdp", "tensor"),
            P("tensor", "fsdp", None, None),
            P("tensor", "fsdp", None, None),
        ),
        check_vma=False,
    )
```

profile of v0, /device:TPU:6, one launch (start us, length us, event | category | flops | bytes accessed | tf_op | source)
XLA Modules:
  0.0 336.9 jit_solution(617230634421711850)
XLA Ops:
  7.2 0.0 copy-start
  7.2 0.0 all-gather.5.cloned.1.call-start
  7.2 0.7 all-gather.5.cloned.1.call-update
  7.9 0.0 all-gather.3.cloned.1.call-start
  8.0 0.7 all-gather.3.cloned.1.call-update
  8.7 0.0 all-reduce.8.cloned.1.call-start
  8.7 1.3 fusion.33
  10.7 0.8 bitcast_dynamic-update-slice_fusion
  11.5 0.7 bitcast_dynamic-update-slice_fusion.1
  12.2 0.7 bitcast_dynamic-update-slice_fusion.2
  13.0 0.7 bitcast_dynamic-update-slice_fusion.3
  13.7 14.9 %all-reduce.5 = (s32[64]{0:T(128)S(1)}, s32[64]{0:T(128)S(1)}, s32[64]{0:T(128)S(1)}, s32[64]{0:T(128)S(1)}) all-reduce(s32[64]{0:T(128)S(1)} %bitcast_dynamic-update-slice_fusion.3, s32[64]{0:T(128)S(1)} %bitcast_dynamic-update-slice_fusion.1, s32[64]{0:T(128)S(1)} %bitcast_dynamic-update-slice_fusion, ...), channel_id=1, replica_groups=mesh['fsdp'=16,'tensor'=16] {'fsdp'}, use_global_device_ids=true, to_apply=%add | all-reduce | flops 256 | bytes 2048 | tf_op jit(solution)/shard_map/broadcast_in_dim;squeeze | solution.py:63
  28.6 0.0 copy-done
  28.7 2.5 copy_bitcast_fusion
  31.2 4.5 %gather_fusion.1 = bf16[64,192,128]{2,1,0:T(8,128)(2,1)} fusion(bf16[192,64,128]{2,0,1:T(8,128)(2,1)} %copy_bitcast_fusion, s32[1024]{0:T(1024)S(1)} %pad_clamp_fusion.2), kind=kCustom, calls=%fused_computation.2.clone | custom fusion | bytes 6291712 | tf_op jit(solution)/shard_map/jit(_take)/gather | solution.py:37
  35.7 2.8 copy_bitcast_fusion.1
  38.4 2.6 gather_fusion
  41.2 21.9 %all-gather.5.cloned.1.call-done = bf16[1,64,128,128]{3,2,0,1:T(8,128)(2,1)} async-done(((bf16[1,4,128,128]{3,2,0,1:T(8,128)(2,1)}), bf16[1,64,128,128]{3,2,0,1:T(8,128)(2,1)}) %all-gather.5.cloned.1.call-update) | async-done | bytes 2097168 | tf_op jit(solution)/shard_map/all_gather | solution.py:28
  63.0 6.2 %fusion.2 = f32[64,192,128]{2,1,0:T(8,128)} fusion(bf16[1,64,128,128]{3,2,0,1:T(8,128)(2,1)} %all-gather.5.cloned.1.call-done, bf16[64,192,128]{2,1,0:T(8,128)(2,1)} %gather_fusion.1, pred[64]{0:T(512)(128)(4,1)S(1)} %get-tuple-element.18), kind=kOutput, calls=%fused_computation.12 | convolution fusion | flops 404226048 | bytes 11534400 | tf_op jit(solution)/shard_map/tsk,skf->stf/dot_general | solution.py:38
  69.2 0.1 broadcast.18.clone
  69.4 10.9 %scatter_fusion.1 = f32[16,192,128]{2,1,0:T(8,128)S(1)} fusion(f32[16,192,128]{2,1,0:T(8,128)S(1)} %broadcast.18.clone, s32[64]{0:T(128)S(1)} %get-tuple-element.8, f32[64,192,128]{2,1,0:T(8,128)} %fusion.2), kind=kCustom, calls=%fused_computation.5 | custom fusion | flops 1572864 | bytes 18874624 | tf_op jit(solution)/shard_map/scatter-add | solution.py:39
  80.3 34.6 %all-gather.3.cloned.1.call-done = bf16[1,64,128,128]{3,2,0,1:T(8,128)(2,1)} async-done(((bf16[1,4,128,128]{3,2,0,1:T(8,128)(2,1)}), bf16[1,64,128,128]{3,2,0,1:T(8,128)(2,1)}) %all-gather.3.cloned.1.call-update) | async-done | bytes 2097168 | tf_op jit(solution)/shard_map/all_gather | solution.py:31
  114.8 6.7 %fusion.6 = f32[64,192,128]{2,1,0:T(8,128)} fusion(bf16[1,64,128,128]{3,2,0,1:T(8,128)(2,1)} %all-gather.3.cloned.1.call-done, bf16[64,192,128]{2,1,0:T(8,128)(2,1)} %gather_fusion, pred[64]{0:T(512)(128)(4,1)S(1)} %compare_and_fusion.3), kind=kOutput, calls=%fused_computation.16 | convolution fusion | flops 404226048 | bytes 11534400 | tf_op jit(solution)/shard_map/tsk,sfk->stf/dot_general | solution.py:44
  121.5 0.1 broadcast.18.clone.1
  121.7 10.6 %scatter_fusion = f32[16,192,128]{2,1,0:T(8,128)S(1)} fusion(f32[16,192,128]{2,1,0:T(8,128)S(1)} %broadcast.18.clone.1, s32[64]{0:T(128)S(1)} %get-tuple-element.6, f32[64,192,128]{2,1,0:T(8,128)} %fusion.6), kind=kCustom, calls=%fused_computation.4 | custom fusion | flops 1572864 | bytes 18874624 | tf_op jit(solution)/shard_map/scatter-add | solution.py:45
  132.3 2.3 multiply_convert_fusion
  134.6 3.7 %gather_fusion.2 = bf16[64,192,128]{2,1,0:T(8,128)(2,1)} fusion(bf16[16,192,128]{2,1,0:T(8,128)(2,1)} %get-tuple-element.12, s32[1024]{0:T(1024)S(1)} %pad_clamp_fusion.1), kind=kCustom, calls=%fused_computation.1.clone | custom fusion | bytes 6291712 | tf_op jit(solution)/shard_map/jit(_take)/gather | solution.py:47
  138.3 0.0 copy-start.2
  138.3 4.5 %convert_bitcast_fusion.1 = bf16[64,1,128,128]{3,2,0,1:T(8,128)(2,1)S(1)} fusion(bf16[64,192,128]{2,1,0:T(8,128)(2,1)} %gather_fusion.1, pred[64]{0:T(512)(128)(4,1)S(1)} %get-tuple-element.18, bf16[64,192,128]{2,1,0:T(8,128)(2,1)} %gather_fusion.2, pred[64]{0:T(512)(128)(4,1)S(1)} %get-tuple-element.17), kind=kOutput, calls=%fused_computation.30 | convolution fusion | flops 406847488 | bytes 8388736 | tf_op jit(solution)/shard_map/tsk,stf->skf/dot_general | solution.py:51
  142.8 0.0 copy-done.2
  142.8 2.6 gather_fusion.3
  145.4 4.4 %convert_bitcast_fusion = bf16[64,1,128,128]{3,2,0,1:T(8,128)(2,1)S(1)} fusion(bf16[64,192,128]{2,1,0:T(8,128)(2,1)} %gather_fusion.3, pred[64]{0:T(512)(128)(4,1)S(1)} %compare_and_fusion, bf16[64,192,128]{2,1,0:T(8,128)(2,1)} %gather_fusion, pred[64]{0:T(512)(128)(4,1)S(1)} %compare_and_fusion.3), kind=kOutput, calls=%fused_computation.29 | convolution fusion | flops 406847488 | bytes 8388736 | tf_op jit(solution)/shard_map/stf,tsk->sfk/dot_general | solution.py:52
  149.9 2.3 pad_maximum_fusion
  152.2 0.0 copy-start.3
  152.2 0.0 all-reduce.8.cloned.1.call-update
  152.2 0.0 reduce-scatter.5.cloned.1.call-start
  152.2 1.8 copy-done.3
  154.0 5.7 %fusion.10 = f32[64,192,128]{2,1,0:T(8,128)} fusion(bf16[1,64,128,128]{3,2,0,1:T(8,128)(2,1)} %all-gather.5.cloned.1.call-done, bf16[64,192,128]{2,1,0:T(8,128)(2,1)S(1)} %copy-done.3, pred[64]{0:T(512)(128)(4,1)S(1)} %get-tuple-element.17), kind=kOutput, calls=%fused_computation.25 | convolution fusion | flops 404226048 | bytes 11534400 | tf_op jit(solution)/shard_map/stf,skf->stk/dot_general | solution.py:62
  159.8 3.6 %broadcast_in_dim.23 = f32[64,192,128]{2,1,0:T(8,128)} broadcast(f32[]{:T(128)} %constant.22.clone.1), dimensions={} | broadcast | bytes 6291460 | tf_op jit(solution)/shard_map/broadcast_in_dim | solution.py:63
  163.4 17.0 %scatter_fusion.2 = f32[64,192,128]{2,1,0:T(8,128)} fusion(f32[64,192,128]{2,1,0:T(8,128)} %broadcast_in_dim.23, s32[64]{0:T(128)S(1)} %get-tuple-element.5, f32[64,192,128]{2,1,0:T(8,128)} %fusion.10), kind=kCustom, calls=%fused_computation.6 | custom fusion | flops 1572864 | bytes 18874624 | tf_op jit(solution)/shard_map/scatter-add | solution.py:63
  180.4 0.0 copy-start.1
  180.4 5.3 %convert_element_type.42 = bf16[64,192,128]{2,1,0:T(8,128)(2,1)} convert(f32[64,192,128]{2,1,0:T(8,128)} %scatter_fusion.2) | non-fusion elementwise | flops 1572864 | bytes 9437184 | tf_op jit(solution)/shard_map/convert_element_type | solution.py:65
  185.7 0.0 reduce-scatter.5.cloned.1.call-update
  186.3 79.4 %all-reduce.8.cloned.1.call-done = bf16[64,2,128,128]{3,2,0,1:T(8,128)(2,1)} async-done(((bf16[64,2,128,128]{3,2,0,1:T(8,128)(2,1)}), bf16[64,2,128,128]{3,2,0,1:T(8,128)(2,1)}) %all-reduce.8.cloned.1.call-update) | async-done | bytes 4194320
  265.7 1.7 dynamic-slice_bitcast_fusion
  267.4 61.4 %reduce-scatter.5.cloned.1.call-done = bf16[4,192,128]{2,1,0:T(8,128)(2,1)} async-done(((bf16[64,192,128]{2,1,0:T(8,128)(2,1)}), bf16[4,192,128]{2,1,0:T(8,128)(2,1)}) %reduce-scatter.5.cloned.1.call-update) | async-done | bytes 196624 | tf_op jit(solution)/shard_map/reduce_scatter | solution.py:64
  328.7 1.6 copy_bitcast_fusion.2
  330.4 0.0 copy-done.1
  (14 shorter events, 0.1 us)
Async XLA Ops:
  7.2 21.5 %copy-start = (bf16[192,8192]{1,0:T(8,128)(2,1)S(1)}, bf16[192,8192]{1,0:T(8,128)(2,1)}, u32[]{:S(2)}) copy-start(bf16[192,8192]{1,0:T(8,128)(2,1)} %param.12) | copy-start | bytes 9437188
  7.2 55.8 %all-gather.5.cloned.1.call-start = ((), (), s32[]{:S(2)}) async-start(), calls=%async_computation.2 | async-start | bytes 2228224 | tf_op jit(solution)/shard_map/all_gather | solution.py:28
  7.9 106.9 %all-gather.3.cloned.1.call-start = ((), (), s32[]{:S(2)}) async-start(), calls=%async_computation.1 | async-start | bytes 2228224 | tf_op jit(solution)/shard_map/all_gather | solution.py:31
  8.7 257.0 %all-reduce.8.cloned.1.call-start = ((), (), s32[]{:S(2)}) async-start(), calls=%async_computation.4 | async-start | bytes 8388608
  138.3 4.5 %copy-start.2 = (bf16[16,192,128]{2,1,0:T(8,128)(2,1)S(1)}, bf16[16,192,128]{2,1,0:T(8,128)(2,1)}, u32[]{:S(2)}) copy-start(bf16[16,192,128]{2,1,0:T(8,128)(2,1)} %get-tuple-element.11) | copy-start | bytes 2359300
  152.2 1.9 copy-start.3
  152.2 176.6 %reduce-scatter.5.cloned.1.call-start = ((), (), s32[]{:S(2)}) async-start(), calls=%async_computation.3 | async-start | bytes 3342336 | tf_op jit(solution)/shard_map/reduce_scatter | solution.py:64
  180.4 150.0 %copy-start.1 = (bf16[192,8192]{1,0:T(8,128)(2,1)S(1)}, bf16[192,8192]{1,0:T(8,128)(2,1)}, u32[]{:S(2)}) copy-start(bf16[192,8192]{1,0:T(8,128)(2,1)} %param.12) | copy-start | bytes 9437188
Sparse Core Ops, SparseCore 0:
  10.4 52.5 all-gather.4
  65.4 49.3 all-gather.2
  152.3 113.3 all-reduce.7
  268.1 60.5 reduce-scatter.4
where the time goes:
time: 338 us; the launch traced here: 337 us
  waiting for transfers between devices  199 us (59%)
  other arithmetic  48.4 us (14%)
  local copies, waits for them, and re-layouts  32.1 us (9%)
  matrix products  27.5 us (8%)
  between operations  15.2 us (4%)
  blocking collectives  14.9 us (4%)
    unnamed x5, waiting for transfers between devices  80.8 us
    reduce_scatter x1, waiting for transfers between devices, on_device(): lax.psum_scatter(in_part.astype(jnp.bfloat16), 'tensor', scatter_dimensio...  61.4 us
    all_gather x1, waiting for transfers between devices, on_device(): lax.all_gather(down_tiles, 'fsdp', axis=1, tiled=True)  34.6 us
    all_gather x1, waiting for transfers between devices, on_device(): lax.all_gather(up_tiles, 'fsdp', axis=1, tiled=True)  21.9 us
    scatter-add x1, other arithmetic, on_device(): in_part = jax.ops.segment_sum(back_in, r_up, num_segments=row_blocks)  17 us
    another operation x1, blocking collectives, on_device(): in_part = jax.ops.segment_sum(back_in, r_up, num_segments=row_blocks)  14.9 us
    scatter-add x1, other arithmetic, on_device(): pre = jax.ops.segment_sum(prod, c_up, num_segments=group_cols)  10.9 us
    scatter-add x1, other arithmetic, on_device(): dhid = jax.ops.segment_sum(back, r_down, num_segments=group_cols)  10.6 us
  transfers between devices with their start and end apart: 4, of which 4 were waited for; matrix products, arithmetic and copies ran while one was open for 20% of the time, Pallas kernels for 0%

commit v1 on v0

v1 whole, which is shorter than its diff:
```python
import jax
import jax.numpy as jnp
from jax import lax
from jax.experimental import pallas as pl
from jax.experimental.pallas import tpu as pltpu
from jax.sharding import PartitionSpec as P

TILE = 128
SLOTS = 64
MESH = pl.DeviceIdType.MESH
F32 = jnp.float32
BF16 = jnp.bfloat16

ORDER = (
    [(0, 0), (0, 3), (0, 1), (0, 2)]
    + [(a, b) for b in (0, 3, 1, 2) for a in (3, 1)]
    + [(2, b) for b in (0, 3, 1, 2)]
)
POS = {ab: n for n, ab in enumerate(ORDER)}
UP_ROW, UP_COL, DN_ROW, DN_COL, PREV_UP, PREV_DN, PREV_ROW, LAST_UP, LAST_DN, LAST_ROW = range(10)


def gelu_parts(pre):
    coef = 0.7978845608028654
    inner = coef * (pre + 0.044715 * pre * pre * pre)
    tanh_val = jnp.tanh(inner)
    act = 0.5 * pre * (1.0 + tanh_val)
    slope = 0.5 * (1.0 + tanh_val) + 0.5 * pre * (1.0 - tanh_val * tanh_val) * coef * (
        1.0 + 3.0 * 0.044715 * pre * pre
    )
    return act, slope


def dot_nn(a, b):
    return lax.dot_general(a, b, (((1,), (0,)), ((), ())), preferred_element_type=F32)


def dot_nt(a, b):
    return lax.dot_general(a, b, (((1,), (1,)), ((), ())), preferred_element_type=F32)


def kernel(
    x_hbm, dy_hbm, up_hbm, down_hbm, ur, uc, dr, dc,
    gin_ref, gup_ref, gdn_ref,
    x_v, dy_v, ga, gb, idx_v, tbl_v, tbl,
    pu, pd, slope_v, dp_v, dpt_v, ht_v,
    pa, pb, ra1, ra2, ra3, ra4, rb1, rb2, rb3, rb4,
    xs, rx, zc, rz,
    send_sem, recv_sem, loc_sem,
):
    f = lax.axis_index("fsdp")
    t = lax.axis_index("tensor")
    y, x = f // 4, f % 4
    z, core = t // 2, t % 2
    xp = {"fsdp": y * 4 + (x + 1) % 4}
    xm = {"fsdp": y * 4 + (x + 3) % 4}
    yp = {"fsdp": ((y + 1) % 4) * 4 + x}
    ym = {"fsdp": ((y + 3) % 4) * 4 + x}
    zp = {"tensor": ((z + 1) % 8) * 2 + core}
    zm = {"tensor": ((z + 7) % 8) * 2 + core}
    mate = {"tensor": z * 2 + 1 - core}

    count = [0]
    sent = []

    def message(src, dst, dev):
        n = count[0]
        count[0] += 1
        copy = pltpu.make_async_remote_copy(
            src_ref=src, dst_ref=dst, send_sem=send_sem.at[n], recv_sem=recv_sem.at[n],
            device_id=dev, device_id_type=MESH,
        )
        sent.append(copy)
        return copy

    own_a = pltpu.make_async_copy(up_hbm.at[0], ga.at[0], loc_sem.at[0])
    own_b = pltpu.make_async_copy(down_hbm.at[0], gb.at[0], loc_sem.at[1])
    get_x = pltpu.make_async_copy(x_v, x_v, loc_sem.at[2])
    get_dy = pltpu.make_async_copy(dy_v, dy_v, loc_sem.at[3])

    def fetch(c, _):
        src = pl.ds(pl.multiple_of(c * TILE, TILE), TILE)
        pltpu.make_async_copy(x_hbm.at[:, src], x_v.at[c], loc_sem.at[2]).start()
        pltpu.make_async_copy(dy_hbm.at[:, src], dy_v.at[c], loc_sem.at[3]).start()
        return 0

    own_a.start()
    own_b.start()

    barrier = pltpu.get_barrier_semaphore()
    for dev in (xp, xm, yp, ym, zp, zm, mate):
        pl.semaphore_signal(barrier, inc=1, device_id=dev, device_id_type=MESH)

    lane = lax.broadcasted_iota(jnp.int32, (8, TILE), 1)
    row = lax.broadcasted_iota(jnp.int32, (8, TILE), 0)
    own = jnp.zeros((8, TILE), jnp.int32)
    for r, ref in enumerate((ur, uc, dr, dc)):
        for i in range(4):
            own = jnp.where((row == r) & (lane == i), ref[0, i], own)
    idx_v[0, 0] = own
    own_a.wait()
    own_b.wait()
    pl.semaphore_wait(barrier, 7)

    class Gather:
        def __init__(self, g, first, second):
            (bp, bm), (ap, am) = first, second
            at = lambda a, b: g.at[POS[a, b]]
            half = lambda a, b, h: g.at[POS[a, b], pl.ds(2 * h, 2)]
            self.f1 = {3: message(at(0, 0), at(0, 3), bp), 1: message(at(0, 0), at(0, 1), bm)}
            self.f2 = {
                3: message(half(0, 3, 0), half(0, 2, 0), bp),
                1: message(half(0, 1, 1), half(0, 2, 1), bm),
            }
            self.s1 = {}
            self.s2 = {}
            for b in (0, 3, 1, 2):
                self.s1[3, b] = message(at(0, b), at(3, b), ap)
                self.s1[1, b] = message(at(0, b), at(1, b), am)
                self.s2[3, b] = message(half(3, b, 0), half(2, b, 0), ap)
                self.s2[1, b] = message(half(1, b, 1), half(2, b, 1), am)

    A = Gather(ga, (xp, xm), (yp, ym))
    B = Gather(gb, (yp, ym), (xp, xm))
    ix = {
        3: message(idx_v.at[0, 0], idx_v.at[0, 3], xp),
        1: message(idx_v.at[0, 0], idx_v.at[0, 1], xm),
        2: message(idx_v.at[0, 3], idx_v.at[0, 2], xp),
    }
    iy = {
        3: message(idx_v.at[0], idx_v.at[3], yp),
        1: message(idx_v.at[0], idx_v.at[1], ym),
        2: message(idx_v.at[3], idx_v.at[2], yp),
    }

    ix[3].start()
    ix[1].start()
    for b in (3, 1):
        A.f1[b].start()
        B.f1[b].start()
    for a in (3, 1):
        A.s1[a, 0].start()
        B.s1[a, 0].start()
    lax.fori_loop(0, 64, fetch, 0)
    ix[3].wait_recv()
    ix[2].start()
    zero = jnp.zeros((192, TILE), F32)
    pu[SLOTS] = zero
    pd[SLOTS] = zero
    ix[1].wait_recv()
    ix[2].wait_recv()
    iy[3].start()
    iy[1].start()

    for b in (3, 1):
        for G in (A, B):
            G.f1[b].wait_recv()
            G.f2[b].start()
            for a in (3, 1):
                G.s1[a, b].start()

    iy[3].wait_recv()
    iy[2].start()
    for G in (A, B):
        for b in (3, 1):
            G.f2[b].wait_recv()
        for a in (3, 1):
            G.s1[a, 2].start()
    iy[1].wait_recv()
    iy[2].wait_recv()

    both = jnp.zeros((8, TILE), jnp.int32)
    for v in range(4):
        for h in range(4):
            tile = idx_v[v, h]
            na, nb = POS[v, h], POS[h, v]
            moved_a = pltpu.roll(tile, 4 * na, 1) if na else tile
            moved_b = pltpu.roll(tile, 4 * nb, 1) if nb else tile
            both = both + jnp.where(row < 2, moved_a, jnp.where(row < 4, moved_b, 0))
    tbl_v[0:8] = both
    si = lax.broadcasted_iota(jnp.int32, (TILE, TILE), 0)
    li = lax.broadcasted_iota(jnp.int32, (TILE, TILE), 1)
    across = lambda r: jnp.broadcast_to(both[r : r + 1], (TILE, TILE))

    def chain(r):
        here = across(r)
        there = here.T
        prev = jnp.max(jnp.where((there == here) & (si < li), si, -1), axis=0, keepdims=True)
        last = jnp.max(jnp.where((there == li) & (si < SLOTS), si, -1), axis=0, keepdims=True)
        fix = lambda v: jnp.where(v < 0, SLOTS, v)
        return fix(prev), fix(last)

    prev_up, last_up = chain(UP_COL)
    prev_dn, last_dn = chain(DN_ROW)
    prev_row, last_row = chain(UP_ROW)
    tbl_v[PREV_UP : PREV_UP + 1] = prev_up
    tbl_v[PREV_DN : PREV_DN + 1] = prev_dn
    tbl_v[PREV_ROW : PREV_ROW + 1] = prev_row
    tbl_v[LAST_UP : LAST_UP + 1] = last_up
    tbl_v[LAST_DN : LAST_DN + 1] = last_dn
    tbl_v[LAST_ROW : LAST_ROW + 1] = last_row
    put = pltpu.make_async_copy(tbl_v, tbl, loc_sem.at[4])
    put.start()
    get_x.wait()
    get_dy.wait()
    put.wait()

    cols = lambda ref, n: ref[n]

    def take_up(n):
        d = []
        for i in range(4):
            s = n * 4 + i
            d.append(dot_nn(cols(x_v, tbl[UP_ROW, s]), ga[n, i]))
        for i in range(4):
            s = n * 4 + i
            pu[s] = d[i] + pu[tbl[PREV_UP, s]]

    def take_down(n):
        d = []
        for i in range(4):
            s = n * 4 + i
            d.append(dot_nt(cols(dy_v, tbl[DN_COL, s]), gb[n, i]))
        for i in range(4):
            s = n * 4 + i
            pd[s] = d[i] + pd[tbl[PREV_DN, s]]

    def take(n, _):
        take_up(n)
        take_down(n)
        return 0

    for k, b in enumerate((0, 3, 1, 2)):
        for G in (A, B):
            for a in (3, 1):
                G.s1[a, b].wait_recv()
                G.s2[a, b].start()
        take(k, 0)
    for k, b in enumerate((0, 3, 1, 2)):
        lax.fori_loop(4 + 2 * k, 6 + 2 * k, take, 0)
    for k, b in enumerate((0, 3, 1, 2)):
        for G in (A, B):
            for a in (3, 1):
                G.s2[a, b].wait_recv()
        take(12 + k, 0)

    def activate(c, _):
        act, slope = gelu_parts(pu[tbl[LAST_UP, c]])
        dpre = pd[tbl[LAST_DN, c]] * slope
        ht_v[c] = act.T.astype(BF16)
        dp_v[c] = dpre.astype(BF16)
        dpt_v[c] = dpre.T.astype(BF16)
        return 0

    lax.fori_loop(0, 16, activate, 0)

    def take_in(n, _):
        d = []
        for i in range(4):
            s = n * 4 + i
            d.append(dot_nt(dp_v[tbl[UP_COL, s]], ga[n, i]))
        for i in range(4):
            s = n * 4 + i
            pu[s] = d[i] + pu[tbl[PREV_ROW, s]]
        return 0

    lax.fori_loop(0, 16, take_in, 0)

    def part(dz, c, j):
        return pu[tbl[LAST_ROW, (((z + dz) % 8) * 2 + c) * 4 + j]]

    ZORDER = (4, 3, 5, 2, 6, 1, 7, 0)
    ex = {dz: message(xs.at[dz], rx.at[dz], mate) for dz in ZORDER}
    for dz in ZORDER:
        for j in range(4):
            xs[dz, j] = part(dz, 1 - core, j).astype(BF16)
        ex[dz].start()

    up_z = {}
    dn_z = {}
    for n in (4, 3, 2, 1):
        for h in range(2):
            hs = pl.ds(2 * h, 2)
            if n < 4 or h == 0:
                up_z[n, h] = message(zc.at[n, hs], rz.at[0, n - 1, hs], zp)
            if n < 4 or h == 1:
                dn_z[n, h] = message(zc.at[8 - n, hs], rz.at[1, n - 1, hs], zm)

    def ring(n):
        if n == 4:
            ex[4].wait_recv()
            for j in range(4):
                zc[4, j] = (part(4, core, j) + rx[4, j].astype(F32)).astype(BF16)
            up_z[4, 0].start()
            dn_z[4, 1].start()
            return
        ex[n].wait_recv()
        ex[8 - n].wait_recv()
        for k in range(2):
            for side, first in ((0, 1), (1, 0)):
                h = first if k == 0 else 1 - first
                came = (up_z, dn_z)[side]
                slot = n if side == 0 else 8 - n
                added = (n + 1, h) in came
                if added:
                    came[n + 1, h].wait_recv()
                for j in (2 * h, 2 * h + 1):
                    v = part(slot, core, j) + rx[slot, j].astype(F32)
                    if added:
                        v = v + rz[side, n, j].astype(F32)
                    zc[slot, j] = v.astype(BF16)
                came[n, h].start()

    def ring_end():
        ex[0].wait_recv()
        for h in range(2):
            up_z[1, h].wait_recv()
            dn_z[1, h].wait_recv()
            for j in (2 * h, 2 * h + 1):
                v = part(0, core, j) + rx[0, j].astype(F32)
                v = v + rz[0, 0, j].astype(F32) + rz[1, 0, j].astype(F32)
                gin_ref[:, j * TILE : (j + 1) * TILE] = v.astype(BF16)

    def grad_up(n):
        for i in range(4):
            s = n * 4 + i
            pa[n, i] = dot_nn(dpt_v[tbl[UP_COL, s]], cols(x_v, tbl[UP_ROW, s])).astype(BF16)

    def grad_down(n):
        for i in range(4):
            s = n * 4 + i
            pb[n, i] = dot_nn(ht_v[tbl[DN_ROW, s]], cols(dy_v, tbl[DN_COL, s])).astype(BF16)

    def add_half(p, n, h, r):
        for i in range(2):
            p[n, 2 * h + i] = (p[n, 2 * h + i].astype(F32) + r[i].astype(F32)).astype(BF16)

    class Scatter:
        def __init__(self, p, r1, r2, r3, r4, grad, first, second):
            (self.ap, self.am), (self.bp, self.bm) = first, second
            self.p, self.r1, self.r2, self.r3, self.r4, self.grad = p, r1, r2, r3, r4, grad
            at = lambda a, b: p.at[POS[a, b]]
            half = lambda a, b, h: p.at[POS[a, b], pl.ds(2 * h, 2)]
            self.m1 = {}
            self.m2 = {}
            for b in range(4):
                self.m1[1, b] = message(half(2, b, 0), r1.at[0, b], self.ap)
                self.m1[3, b] = message(half(2, b, 1), r1.at[1, b], self.am)
                self.m2[1, b] = message(at(1, b), r2.at[0, b], self.ap)
                self.m2[3, b] = message(at(3, b), r2.at[1, b], self.am)
            self.m3 = {
                1: message(half(0, 2, 0), r3.at[0], self.bp),
                3: message(half(0, 2, 1), r3.at[1], self.bm),
            }
            self.m4 = {
                1: message(at(0, 1), r4.at[0], self.bp),
                3: message(at(0, 3), r4.at[1], self.bm),
            }

        def far(self, b):
            self.grad(POS[2, b])
            self.m1[1, b].start()
            self.m1[3, b].start()

        def near(self, a, b):
            self.grad(POS[a, b])
            self.m1[a, b].wait_recv()
            h = 0 if a == 1 else 1
            add_half(self.p, POS[a, b], h, self.r1.at[h, b])
            self.m2[a, b].start()

        def total(self, b):
            self.m2[1, b].wait_recv()
            self.m2[3, b].wait_recv()
            n = POS[0, b]
            for i in range(4):
                v = self.p[n, i].astype(F32) + self.r2[0, b, i].astype(F32)
                v = v + self.r2[1, b, i].astype(F32)
                self.p[n, i] = v.astype(BF16)
            if b == 2:
                self.m3[1].start()
                self.m3[3].start()

        def turn(self, b):
            h = 0 if b == 1 else 1
            self.m3[b].wait_recv()
            add_half(self.p, POS[0, b], h, self.r3.at[h])
            self.m4[b].start()

        def end(self, out, flip):
            self.m4[1].wait_recv()
            self.m4[3].wait_recv()
            for i in range(4):
                v = self.p[POS[0, 0], i].astype(F32) + self.r4[0, i].astype(F32)
                v = v + self.r4[1, i].astype(F32)
                out[0, i] = (v.T if flip else v).astype(BF16)

    U = Scatter(pa, ra1, ra2, ra3, ra4, grad_up, (yp, ym), (xp, xm))
    D = Scatter(pb, rb1, rb2, rb3, rb4, grad_down, (xp, xm), (yp, ym))

    for b in (2, 1, 3, 0):
        U.far(b)
        D.far(b)
    ring(4)
    for b in (2, 1):
        for a in (1, 3):
            U.near(a, b)
            D.near(a, b)
    ring(3)
    for b in (3, 0):
        for a in (1, 3):
            U.near(a, b)
            D.near(a, b)
    ring(2)
    for b in (2, 1, 3, 0):
        grad_up(POS[0, b])
        grad_down(POS[0, b])
    for S in (U, D):
        S.total(2)
    ring(1)
    for b in (1, 3):
        for S in (U, D):
            S.total(b)
            S.turn(b)
    for S in (U, D):
        S.total(0)
    ring_end()
    U.end(gup_ref, True)
    D.end(gdn_ref, False)
    for copy in sent:
        copy.wait_send()
    assert count[0] <= 128


def on_device(inputs, cotangent, up_tiles, up_rows, up_cols, down_tiles, down_rows, down_cols):
    tok = inputs.shape[0]
    width = inputs.shape[1]
    hbm = pl.BlockSpec(memory_space=pl.ANY)
    vmem = pl.BlockSpec(memory_space=pltpu.VMEM)
    smem = pl.BlockSpec(memory_space=pltpu.SMEM)
    tiles = lambda *n: pltpu.VMEM((*n, TILE, TILE), BF16)
    blocks = lambda *n: pltpu.VMEM((*n, tok, TILE), BF16)
    scatter_bufs = [tiles(2, 4, 2), tiles(2, 4, 4), tiles(2, 2), tiles(2, 4)]
    return pl.pallas_call(
        kernel,
        out_shape=(
            jax.ShapeDtypeStruct((tok, 4 * TILE), BF16),
            jax.ShapeDtypeStruct((1, 4, TILE, TILE), BF16),
            jax.ShapeDtypeStruct((1, 4, TILE, TILE), BF16),
        ),
        in_specs=[hbm, hbm, hbm, hbm, smem, smem, smem, smem],
        out_specs=(vmem, vmem, vmem),
        scratch_shapes=[
            blocks(width // TILE),
            blocks(width // TILE),
            tiles(16, 4),
            tiles(16, 4),
            pltpu.VMEM((4, 4, 8, TILE), jnp.int32),
            pltpu.VMEM((16, TILE), jnp.int32),
            pltpu.SMEM((16, TILE), jnp.int32),
            pltpu.VMEM((SLOTS + 1, tok, TILE), F32),
            pltpu.VMEM((SLOTS + 1, tok, TILE), F32),
            pltpu.VMEM((8, TILE), F32),
            blocks(16),
            pltpu.VMEM((16, TILE, tok), BF16),
            pltpu.VMEM((16, TILE, tok), BF16),
            tiles(16, 4),
            tiles(16, 4),
            *scatter_bufs,
            *scatter_bufs,
            blocks(8, 4),
            blocks(8, 4),
            blocks(8, 4),
            blocks(2, 4, 4),
            pltpu.SemaphoreType.DMA((128,)),
            pltpu.SemaphoreType.DMA((128,)),
            pltpu.SemaphoreType.DMA((8,)),
        ],
        compiler_params=pltpu.CompilerParams(
            collective_id=0, has_side_effects=True, vmem_limit_bytes=60 * 1024 * 1024
        ),
    )(inputs, cotangent, up_tiles, down_tiles, up_rows, up_cols, down_rows, down_cols)


def solution(mesh):
    placed = (
        P("fsdp", None),
        P("fsdp", None),
        P("tensor", "fsdp", None, None),
        P("tensor", "fsdp"),
        P("tensor", "fsdp"),
        P("tensor", "fsdp", None, None),
        P("tensor", "fsdp"),
        P("tensor", "fsdp"),
    )
    return jax.shard_map(
        on_device,
        mesh=mesh,
        in_specs=placed,
        out_specs=(
            P("fsdp", "tensor"),
            P("tensor", "fsdp", None, None),
            P("tensor", "fsdp", None, None),
        ),
        check_vma=False,
    )
```

time: 338 us -> 74.2 us (0.22)
  waiting for transfers between devices: 199 us -> 0 us
  Pallas kernels: 0 us -> 68.6 us
  other arithmetic: 48.4 us -> 0 us
  matrix products: 27.5 us -> 0 us
  local copies, waits for them, and re-layouts: 32.1 us -> 4.75 us
  blocking collectives: 14.9 us -> 0 us
  between operations: 15.2 us -> 0.64 us
    unnamed x5 -> x0, waiting for transfers between devices: 80.8 us -> none
    pallas_call x0 -> x1, Pallas kernels: none -> 68.6 us  [on_device(): pl.pallas_call(kernel, out_shape=(jax.ShapeDtypeStruct((tok, 4 * TILE), B...]
    reduce_scatter x1 -> x0, waiting for transfers between devices: 61.4 us -> none  [on_device(): lax.psum_scatter(in_part.astype(jnp.bfloat16), 'tensor', scatter_dimensio...]
    all_gather x2 -> x0, waiting for transfers between devices: 56.4 us -> none  [the longest x1 34.6 us: on_device(): lax.all_gather(down_tiles, 'fsdp', axis=1, tiled=True)]
    scatter-add x3 -> x0, other arithmetic: 38.5 us -> none  [the longest x1 17 us: on_device(): in_part = jax.ops.segment_sum(back_in, r_up, num_segments=row_blocks)]
    dot_general x5 -> x0, matrix products: 27.5 us -> none  [the longest x1 6.7 us: on_device(): jnp.einsum('tsk,sfk->stf', dy_sel, w_down, preferred_element_type=jnp.flo...]
    another operation x1 -> x0, blocking collectives: 14.9 us -> none  [on_device(): in_part = jax.ops.segment_sum(back_in, r_up, num_segments=row_blocks)]
    gather x4 -> x0, local copies, waits for them, and re-layouts: 13.5 us -> none  [the longest x1 4.47 us: on_device(): x_sel = jnp.take(input_blocks, r_up, axis=1)]
  transfers between devices with their start and end apart: 4 -> 0, of which waited for: 4 -> 0; matrix products, arithmetic and copies ran while one was open for 20% -> 0% of each run, Pallas kernels for 0% -> 0%
where the time goes in v1:
time: 74.2 us; the launch traced here: 74 us
  Pallas kernels  68.6 us (92%)
  local copies, waits for them, and re-layouts  4.75 us (6%)
    pallas_call x1, Pallas kernels, on_device(): pl.pallas_call(kernel, out_shape=(jax.ShapeDtypeStruct((tok, 4 * TILE), B...  68.6 us
    unnamed x3, local copies, waits for them, and re-layouts  4.75 us

profile of v1, /device:TPU:6, one launch (start us, length us, event | category | flops | bytes accessed | tf_op | source)
XLA Modules:
  0.0 74.0 jit_solution(10158783065955271520)
XLA Ops:
  0.6 68.6 %shard_map.103 = (bf16[192,512]{1,0:T(8,128)(2,1)}, bf16[1,4,128,128]{3,2,1,0:T(8,128)(2,1)}, bf16[1,4,128,128]{3,2,1,0:T(8,128)(2,1)}) custom-call(bf16[192,8192]{1,0:T(8,128)(2,1)} %x_hbm.1, bf16[192,8192]{1,0:T(8,128)(2,1)} %dy_hbm.1, bf16[1,4,128,128]{3,2,1,0:T(8,128)(2,1)} %up_hbm.1, bf16[1,4,128,128]{3,2,1,0:T(8,128)(2,1)} %down_hbm.1, s32[1,4]{1,0:T(1,128)} %ur.1, ...), custom_call_target="tpu_custom_call" | custom-call | tf_op jit(solution)/shard_map/pallas_call | solution.py:444
  69.2 1.6 %copy.14 = bf16[192,512]{1,0:T(8,128)(2,1)} copy(bf16[192,512]{1,0:T(8,128)(2,1)} %get-tuple-element.6) | data formatting | bytes 393216
  70.9 1.6 %copy.15 = bf16[1,4,128,128]{3,2,1,0:T(8,128)(2,1)} copy(bf16[1,4,128,128]{3,2,1,0:T(8,128)(2,1)} %get-tuple-element.7) | data formatting | bytes 262144
  72.4 1.6 %copy.16 = bf16[1,4,128,128]{3,2,1,0:T(8,128)(2,1)} copy(bf16[1,4,128,128]{3,2,1,0:T(8,128)(2,1)} %get-tuple-element.8) | data formatting | bytes 262144

commit v2 on v1

--- a/solution.py
+++ b/solution.py
@@ -103,25 +103,58 @@
     pl.semaphore_wait(barrier, 7)
 
     class Gather:
-        def __init__(self, g, first, second):
-            (bp, bm), (ap, am) = first, second
-            at = lambda a, b: g.at[POS[a, b]]
-            half = lambda a, b, h: g.at[POS[a, b], pl.ds(2 * h, 2)]
-            self.f1 = {3: message(at(0, 0), at(0, 3), bp), 1: message(at(0, 0), at(0, 1), bm)}
-            self.f2 = {
-                3: message(half(0, 3, 0), half(0, 2, 0), bp),
-                1: message(half(0, 1, 1), half(0, 2, 1), bm),
-            }
-            self.s1 = {}
-            self.s2 = {}
-            for b in (0, 3, 1, 2):
-                self.s1[3, b] = message(at(0, b), at(3, b), ap)
-                self.s1[1, b] = message(at(0, b), at(1, b), am)
-                self.s2[3, b] = message(half(3, b, 0), half(2, b, 0), ap)
-                self.s2[1, b] = message(half(1, b, 1), half(2, b, 1), am)
-
-    A = Gather(ga, (xp, xm), (yp, ym))
-    B = Gather(gb, (yp, ym), (xp, xm))
+        def __init__(self, g):
+            self.own_first, self.own_second = [], []
+            self.f1, self.f2, self.s1, self.s2 = {}, {}, {}, {}
+            for o, bp, bm, ap, am in ((0, xp, xm, yp, ym), (2, yp, ym, xp, xm)):
+                at = lambda a, b: g.at[POS[a, b], pl.ds(o, 2)]
+                half = lambda a, b, h: g.at[POS[a, b], pl.ds(o + h, 1)]
+                self.f1[o, 3] = message(at(0, 0), at(0, 3), bp)
+                self.f1[o, 1] = message(at(0, 0), at(0, 1), bm)
+                self.f2[o, 3] = message(half(0, 3, 0), half(0, 2, 0), bp)
+                self.f2[o, 1] = message(half(0, 1, 1), half(0, 2, 1), bm)
+                for b in (0, 3, 1, 2):
+                    self.s1[o, 3, b] = message(at(0, b), at(3, b), ap)
+                    self.s1[o, 1, b] = message(at(0, b), at(1, b), am)
+                    self.s2[o, 3, b] = message(half(3, b, 0), half(2, b, 0), ap)
+                    self.s2[o, 1, b] = message(half(1, b, 1), half(2, b, 1), am)
+
+        def send_first(self):
+            for b in (3, 1):
+                for o in (0, 2):
+                    self.f1[o, b].start()
+
+        def send_second(self, b):
+            for a in (3, 1):
+                for o in (0, 2):
+                    self.s1[o, a, b].start()
+
+        def turn(self):
+            for b in (3, 1):
+                for o in (0, 2):
+                    self.f1[o, b].wait_recv()
+                    self.f2[o, b].start()
+                self.send_second(b)
+
+        def opposite(self):
+            for b in (3, 1):
+                for o in (0, 2):
+                    self.f2[o, b].wait_recv()
+            self.send_second(2)
+
+        def forward(self, b):
+            for a in (3, 1):
+                for o in (0, 2):
+                    self.s1[o, a, b].wait_recv()
+                    self.s2[o, a, b].start()
+
+        def close(self, b):
+            for a in (3, 1):
+                for o in (0, 2):
+                    self.s2[o, a, b].wait_recv()
+
+    A = Gather(ga)
+    B = Gather(gb)
     ix = {
         3: message(idx_v.at[0, 0], idx_v.at[0, 3], xp),
         1: message(idx_v.at[0, 0], idx_v.at[0, 1], xm),
@@ -135,12 +168,8 @@
 
     ix[3].start()
     ix[1].start()
-    for b in (3, 1):
-        A.f1[b].start()
-        B.f1[b].start()
-    for a in (3, 1):
-        A.s1[a, 0].start()
-        B.s1[a, 0].start()
+    A.send_first()
+    A.send_second(0)
     lax.fori_loop(0, 64, fetch, 0)
     ix[3].wait_recv()
     ix[2].start()
@@ -151,32 +180,23 @@
     ix[2].wait_recv()
     iy[3].start()
     iy[1].start()
-
-    for b in (3, 1):
-        for G in (A, B):
-            G.f1[b].wait_recv()
-            G.f2[b].start()
-            for a in (3, 1):
-                G.s1[a, b].start()
-
+    A.turn()
     iy[3].wait_recv()
     iy[2].start()
-    for G in (A, B):
-        for b in (3, 1):
-            G.f2[b].wait_recv()
-        for a in (3, 1):
-            G.s1[a, 2].start()
+    A.opposite()
+    B.send_first()
     iy[1].wait_recv()
     iy[2].wait_recv()
 
     both = jnp.zeros((8, TILE), jnp.int32)
+    early = (lane & 3) < 2
     for v in range(4):
         for h in range(4):
             tile = idx_v[v, h]
             na, nb = POS[v, h], POS[h, v]
             moved_a = pltpu.roll(tile, 4 * na, 1) if na else tile
             moved_b = pltpu.roll(tile, 4 * nb, 1) if nb else tile
-            both = both + jnp.where(row < 2, moved_a, jnp.where(row < 4, moved_b, 0))
+            both = both + jnp.where(early, moved_a, moved_b)
     tbl_v[0:8] = both
     si = lax.broadcasted_iota(jnp.int32, (TILE, TILE), 0)
     li = lax.broadcasted_iota(jnp.int32, (TILE, TILE), 1)
@@ -225,34 +245,128 @@
             s = n * 4 + i
             pd[s] = d[i] + pd[tbl[PREV_DN, s]]
 
-    def take(n, _):
-        take_up(n)
-        take_down(n)
-        return 0
+    def grad_up(n):
+        for i in range(4):
+            s = n * 4 + i
+            pa[n, i] = dot_nn(dpt_v[tbl[UP_COL, s]], cols(x_v, tbl[UP_ROW, s])).astype(BF16)
+
+    def grad_down(n):
+        for i in range(4):
+            s = n * 4 + i
+            pb[n, i] = dot_nn(ht_v[tbl[DN_ROW, s]], cols(dy_v, tbl[DN_COL, s])).astype(BF16)
+
+    def looped(first, end, step):
+        def body(n, _):
+            step(n)
+            return 0
+
+        lax.fori_loop(first, end, body, 0)
+
+    def add_tile(p, n, s, r):
+        p[n, s] = (p[n, s].astype(F32) + r.astype(F32)).astype(BF16)
+
+    class Scatter:
+        def __init__(self, p, r1, r2, r3, r4):
+            self.p, self.r1, self.r2, self.r3, self.r4 = p, r1, r2, r3, r4
+            self.m1, self.m2, self.m3, self.m4 = {}, {}, {}, {}
+            for o, ap, am, bp, bm in ((0, yp, ym, xp, xm), (2, xp, xm, yp, ym)):
+                at = lambda a, b: p.at[POS[a, b], pl.ds(o, 2)]
+                half = lambda a, b, h: p.at[POS[a, b], pl.ds(o + h, 1)]
+                k = o // 2
+                for b in range(4):
+                    self.m1[o, 1, b] = message(half(2, b, 0), r1.at[k, 0, b], ap)
+                    self.m1[o, 3, b] = message(half(2, b, 1), r1.at[k, 1, b], am)
+                    self.m2[o, 1, b] = message(at(1, b), r2.at[k, 0, b], ap)
+                    self.m2[o, 3, b] = message(at(3, b), r2.at[k, 1, b], am)
+                self.m3[o, 1] = message(half(0, 2, 0), r3.at[k, 0], bp)
+                self.m3[o, 3] = message(half(0, 2, 1), r3.at[k, 1], bm)
+                self.m4[o, 1] = message(at(0, 1), r4.at[k, 0], bp)
+                self.m4[o, 3] = message(at(0, 3), r4.at[k, 1], bm)
+
+        def far(self, b):
+            for a in (1, 3):
+                for o in (0, 2):
+                    self.m1[o, a, b].start()
+
+        def near(self, a, b):
+            h = 0 if a == 1 else 1
+            for o in (0, 2):
+                self.m1[o, a, b].wait_recv()
+                add_tile(self.p, POS[a, b], o + h, self.r1[o // 2, h, b, 0])
+                self.m2[o, a, b].start()
+
+        def total(self, b):
+            n = POS[0, b]
+            for o in (0, 2):
+                self.m2[o, 1, b].wait_recv()
+                self.m2[o, 3, b].wait_recv()
+                for i in range(2):
+                    v = self.p[n, o + i].astype(F32) + self.r2[o // 2, 0, b, i].astype(F32)
+                    v = v + self.r2[o // 2, 1, b, i].astype(F32)
+                    self.p[n, o + i] = v.astype(BF16)
+                if b == 2:
+                    self.m3[o, 1].start()
+                    self.m3[o, 3].start()
+
+        def turn(self, b):
+            h = 0 if b == 1 else 1
+            for o in (0, 2):
+                self.m3[o, b].wait_recv()
+                add_tile(self.p, POS[0, b], o + h, self.r3[o // 2, h, 0])
+                self.m4[o, b].start()
+
+        def end(self, out, flip):
+            for o in (0, 2):
+                self.m4[o, 1].wait_recv()
+                self.m4[o, 3].wait_recv()
+                for i in range(2):
+                    v = self.p[POS[0, 0], o + i].astype(F32) + self.r4[o // 2, 0, i].astype(F32)
+                    v = v + self.r4[o // 2, 1, i].astype(F32)
+                    out[0, o + i] = (v.T if flip else v).astype(BF16)
+
+    U = Scatter(pa, ra1, ra2, ra3, ra4)
+    D = Scatter(pb, rb1, rb2, rb3, rb4)
 
     for k, b in enumerate((0, 3, 1, 2)):
-        for G in (A, B):
-            for a in (3, 1):
-                G.s1[a, b].wait_recv()
-                G.s2[a, b].start()
-        take(k, 0)
+        A.forward(b)
+        if k == 1:
+            B.send_second(0)
+        take_up(k)
+    B.turn()
+    looped(4, 12, take_up)
+    B.opposite()
     for k, b in enumerate((0, 3, 1, 2)):
-        lax.fori_loop(4 + 2 * k, 6 + 2 * k, take, 0)
+        A.close(b)
+        take_up(12 + k)
+    B.forward(0)
+
+    def activate(c):
+        act, slope = gelu_parts(pu[tbl[LAST_UP, c]])
+        slope_v[c] = slope
+        ht_v[c] = act.T.astype(BF16)
+
+    looped(0, 16, activate)
+
+    for b in (3, 1, 2):
+        B.forward(b)
+    for b in (2, 1, 3, 0):
+        grad_down(POS[2, b])
+        D.far(b)
+    looped(0, 12, take_down)
+    looped(0, 12, grad_down)
     for k, b in enumerate((0, 3, 1, 2)):
-        for G in (A, B):
-            for a in (3, 1):
-                G.s2[a, b].wait_recv()
-        take(12 + k, 0)
-
-    def activate(c, _):
-        act, slope = gelu_parts(pu[tbl[LAST_UP, c]])
-        dpre = pd[tbl[LAST_DN, c]] * slope
-        ht_v[c] = act.T.astype(BF16)
+        B.close(b)
+        take_down(12 + k)
+
+    def back(c):
+        dpre = pd[tbl[LAST_DN, c]] * slope_v[c]
         dp_v[c] = dpre.astype(BF16)
         dpt_v[c] = dpre.T.astype(BF16)
-        return 0
-
-    lax.fori_loop(0, 16, activate, 0)
+
+    looped(0, 16, back)
+    for b in (2, 1, 3, 0):
+        grad_up(POS[2, b])
+        U.far(b)
 
     def take_in(n, _):
         d = []
@@ -321,100 +435,21 @@
                 v = v + rz[0, 0, j].astype(F32) + rz[1, 0, j].astype(F32)
                 gin_ref[:, j * TILE : (j + 1) * TILE] = v.astype(BF16)
 
-    def grad_up(n):
-        for i in range(4):
-            s = n * 4 + i
-            pa[n, i] = dot_nn(dpt_v[tbl[UP_COL, s]], cols(x_v, tbl[UP_ROW, s])).astype(BF16)
-
-    def grad_down(n):
-        for i in range(4):
-            s = n * 4 + i
-            pb[n, i] = dot_nn(ht_v[tbl[DN_ROW, s]], cols(dy_v, tbl[DN_COL, s])).astype(BF16)
-
-    def add_half(p, n, h, r):
-        for i in range(2):
-            p[n, 2 * h + i] = (p[n, 2 * h + i].astype(F32) + r[i].astype(F32)).astype(BF16)
-
-    class Scatter:
-        def __init__(self, p, r1, r2, r3, r4, grad, first, second):
-            (self.ap, self.am), (self.bp, self.bm) = first, second
-            self.p, self.r1, self.r2, self.r3, self.r4, self.grad = p, r1, r2, r3, r4, grad
-            at = lambda a, b: p.at[POS[a, b]]
-            half = lambda a, b, h: p.at[POS[a, b], pl.ds(2 * h, 2)]
-            self.m1 = {}
-            self.m2 = {}
-            for b in range(4):
-                self.m1[1, b] = message(half(2, b, 0), r1.at[0, b], self.ap)
-                self.m1[3, b] = message(half(2, b, 1), r1.at[1, b], self.am)
-                self.m2[1, b] = message(at(1, b), r2.at[0, b], self.ap)
-                self.m2[3, b] = message(at(3, b), r2.at[1, b], self.am)
-            self.m3 = {
-                1: message(half(0, 2, 0), r3.at[0], self.bp),
-                3: message(half(0, 2, 1), r3.at[1], self.bm),
-            }
-            self.m4 = {
-                1: message(at(0, 1), r4.at[0], self.bp),
-                3: message(at(0, 3), r4.at[1], self.bm),
-            }
-
-        def far(self, b):
-            self.grad(POS[2, b])
-            self.m1[1, b].start()
-            self.m1[3, b].start()
-
-        def near(self, a, b):
-            self.grad(POS[a, b])
-            self.m1[a, b].wait_recv()
-            h = 0 if a == 1 else 1
-            add_half(self.p, POS[a, b], h, self.r1.at[h, b])
-            self.m2[a, b].start()
-
-        def total(self, b):
-            self.m2[1, b].wait_recv()
-            self.m2[3, b].wait_recv()
-            n = POS[0, b]
-            for i in range(4):
-                v = self.p[n, i].astype(F32) + self.r2[0, b, i].astype(F32)
-                v = v + self.r2[1, b, i].astype(F32)
-                self.p[n, i] = v.astype(BF16)
-            if b == 2:
-                self.m3[1].start()
-                self.m3[3].start()
-
-        def turn(self, b):
-            h = 0 if b == 1 else 1
-            self.m3[b].wait_recv()
-            add_half(self.p, POS[0, b], h, self.r3.at[h])
-            self.m4[b].start()
-
-        def end(self, out, flip):
-            self.m4[1].wait_recv()
-            self.m4[3].wait_recv()
-            for i in range(4):
-                v = self.p[POS[0, 0], i].astype(F32) + self.r4[0, i].astype(F32)
-                v = v + self.r4[1, i].astype(F32)
-                out[0, i] = (v.T if flip else v).astype(BF16)
-
-    U = Scatter(pa, ra1, ra2, ra3, ra4, grad_up, (yp, ym), (xp, xm))
-    D = Scatter(pb, rb1, rb2, rb3, rb4, grad_down, (xp, xm), (yp, ym))
-
-    for b in (2, 1, 3, 0):
-        U.far(b)
-        D.far(b)
     ring(4)
     for b in (2, 1):
         for a in (1, 3):
+            grad_up(POS[a, b])
             U.near(a, b)
             D.near(a, b)
     ring(3)
     for b in (3, 0):
         for a in (1, 3):
+            grad_up(POS[a, b])
             U.near(a, b)
             D.near(a, b)
     ring(2)
     for b in (2, 1, 3, 0):
         grad_up(POS[0, b])
-        grad_down(POS[0, b])
     for S in (U, D):
         S.total(2)
     ring(1)
@@ -429,7 +464,7 @@
     D.end(gdn_ref, False)
     for copy in sent:
         copy.wait_send()
-    assert count[0] <= 128
+    assert count[0] <= 192
 
 
 def on_device(inputs, cotangent, up_tiles, up_rows, up_cols, down_tiles, down_rows, down_cols):
@@ -440,7 +475,7 @@
     smem = pl.BlockSpec(memory_space=pltpu.SMEM)
     tiles = lambda *n: pltpu.VMEM((*n, TILE, TILE), BF16)
     blocks = lambda *n: pltpu.VMEM((*n, tok, TILE), BF16)
-    scatter_bufs = [tiles(2, 4, 2), tiles(2, 4, 4), tiles(2, 2), tiles(2, 4)]
+    scatter_bufs = [tiles(2, 2, 4, 1), tiles(2, 2, 4, 2), tiles(2, 2, 1), tiles(2, 2, 2)]
     return pl.pallas_call(
         kernel,
         out_shape=(
@@ -460,7 +495,7 @@
             pltpu.SMEM((16, TILE), jnp.int32),
             pltpu.VMEM((SLOTS + 1, tok, TILE), F32),
             pltpu.VMEM((SLOTS + 1, tok, TILE), F32),
-            pltpu.VMEM((8, TILE), F32),
+            pltpu.VMEM((16, tok, TILE), F32),
             blocks(16),
             pltpu.VMEM((16, TILE, tok), BF16),
             pltpu.VMEM((16, TILE, tok), BF16),
@@ -472,8 +507,8 @@
             blocks(8, 4),
             blocks(8, 4),
             blocks(2, 4, 4),
-            pltpu.SemaphoreType.DMA((128,)),
-            pltpu.SemaphoreType.DMA((128,)),
+            pltpu.SemaphoreType.DMA((192,)),
+            pltpu.SemaphoreType.DMA((192,)),
             pltpu.SemaphoreType.DMA((8,)),
         ],
         compiler_params=pltpu.CompilerParams(

time: 74.2 us -> 81.6 us (1.100)
  the two profiles are of different devices: /device:TPU:6 before, /device:TPU:1 now
where the time goes in v2:
time: 81.6 us; the launch traced here: 81.5 us
  Pallas kernels  76.1 us (93%)
  local copies, waits for them, and re-layouts  4.75 us (6%)
    pallas_call x1, Pallas kernels, on_device(): pl.pallas_call(kernel, out_shape=(jax.ShapeDtypeStruct((tok, 4 * TILE), B...  76.1 us
    unnamed x3, local copies, waits for them, and re-layouts  4.75 us

profile of v2, /device:TPU:1, one launch (start us, length us, event | category | flops | bytes accessed | tf_op | source)
XLA Modules:
  0.0 81.5 jit_solution(11169775164095538272)
XLA Ops:
  0.6 76.1 %shard_map.103 = (bf16[192,512]{1,0:T(8,128)(2,1)}, bf16[1,4,128,128]{3,2,1,0:T(8,128)(2,1)}, bf16[1,4,128,128]{3,2,1,0:T(8,128)(2,1)}) custom-call(bf16[192,8192]{1,0:T(8,128)(2,1)} %x_hbm.1, bf16[192,8192]{1,0:T(8,128)(2,1)} %dy_hbm.1, bf16[1,4,128,128]{3,2,1,0:T(8,128)(2,1)} %up_hbm.1, bf16[1,4,128,128]{3,2,1,0:T(8,128)(2,1)} %down_hbm.1, s32[1,4]{1,0:T(1,128)} %ur.1, ...), custom_call_target="tpu_custom_call" | custom-call | tf_op jit(solution)/shard_map/pallas_call | solution.py:479
  76.7 1.6 %copy.14 = bf16[192,512]{1,0:T(8,128)(2,1)} copy(bf16[192,512]{1,0:T(8,128)(2,1)} %get-tuple-element.6) | data formatting | bytes 393216
  78.3 1.6 %copy.15 = bf16[1,4,128,128]{3,2,1,0:T(8,128)(2,1)} copy(bf16[1,4,128,128]{3,2,1,0:T(8,128)(2,1)} %get-tuple-element.7) | data formatting | bytes 262144
  79.9 1.6 %copy.16 = bf16[1,4,128,128]{3,2,1,0:T(8,128)(2,1)} copy(bf16[1,4,128,128]{3,2,1,0:T(8,128)(2,1)} %get-tuple-element.8) | data formatting | bytes 262144

commit v3 on v1

--- a/solution.py
+++ b/solution.py
@@ -84,12 +84,11 @@
         pltpu.make_async_copy(dy_hbm.at[:, src], dy_v.at[c], loc_sem.at[3]).start()
         return 0
 
-    own_a.start()
-    own_b.start()
-
     barrier = pltpu.get_barrier_semaphore()
     for dev in (xp, xm, yp, ym, zp, zm, mate):
         pl.semaphore_signal(barrier, inc=1, device_id=dev, device_id_type=MESH)
+    own_a.start()
+    own_b.start()
 
     lane = lax.broadcasted_iota(jnp.int32, (8, TILE), 1)
     row = lax.broadcasted_iota(jnp.int32, (8, TILE), 0)
@@ -98,16 +97,14 @@
         for i in range(4):
             own = jnp.where((row == r) & (lane == i), ref[0, i], own)
     idx_v[0, 0] = own
-    own_a.wait()
-    own_b.wait()
     pl.semaphore_wait(barrier, 7)
 
     class Gather:
-        def __init__(self, g, first, second):
+        def __init__(self, g, own, first, second):
             (bp, bm), (ap, am) = first, second
             at = lambda a, b: g.at[POS[a, b]]
             half = lambda a, b, h: g.at[POS[a, b], pl.ds(2 * h, 2)]
-            self.f1 = {3: message(at(0, 0), at(0, 3), bp), 1: message(at(0, 0), at(0, 1), bm)}
+            self.f1 = {3: message(own, at(0, 3), bp), 1: message(own, at(0, 1), bm)}
             self.f2 = {
                 3: message(half(0, 3, 0), half(0, 2, 0), bp),
                 1: message(half(0, 1, 1), half(0, 2, 1), bm),
@@ -115,13 +112,14 @@
             self.s1 = {}
             self.s2 = {}
             for b in (0, 3, 1, 2):
-                self.s1[3, b] = message(at(0, b), at(3, b), ap)
-                self.s1[1, b] = message(at(0, b), at(1, b), am)
+                src = at(0, b) if b else own
+                self.s1[3, b] = message(src, at(3, b), ap)
+                self.s1[1, b] = message(src, at(1, b), am)
                 self.s2[3, b] = message(half(3, b, 0), half(2, b, 0), ap)
                 self.s2[1, b] = message(half(1, b, 1), half(2, b, 1), am)
 
-    A = Gather(ga, (xp, xm), (yp, ym))
-    B = Gather(gb, (yp, ym), (xp, xm))
+    A = Gather(ga, up_hbm.at[0], (xp, xm), (yp, ym))
+    B = Gather(gb, down_hbm.at[0], (yp, ym), (xp, xm))
     ix = {
         3: message(idx_v.at[0, 0], idx_v.at[0, 3], xp),
         1: message(idx_v.at[0, 0], idx_v.at[0, 1], xm),
@@ -203,6 +201,8 @@
     put.start()
     get_x.wait()
     get_dy.wait()
+    own_a.wait()
+    own_b.wait()
     put.wait()
 
     cols = lambda ref, n: ref[n]
@@ -244,37 +244,11 @@
                 G.s2[a, b].wait_recv()
         take(12 + k, 0)
 
-    def activate(c, _):
-        act, slope = gelu_parts(pu[tbl[LAST_UP, c]])
-        dpre = pd[tbl[LAST_DN, c]] * slope
-        ht_v[c] = act.T.astype(BF16)
-        dp_v[c] = dpre.astype(BF16)
-        dpt_v[c] = dpre.T.astype(BF16)
-        return 0
-
-    lax.fori_loop(0, 16, activate, 0)
-
-    def take_in(n, _):
-        d = []
-        for i in range(4):
-            s = n * 4 + i
-            d.append(dot_nt(dp_v[tbl[UP_COL, s]], ga[n, i]))
-        for i in range(4):
-            s = n * 4 + i
-            pu[s] = d[i] + pu[tbl[PREV_ROW, s]]
-        return 0
-
-    lax.fori_loop(0, 16, take_in, 0)
-
     def part(dz, c, j):
         return pu[tbl[LAST_ROW, (((z + dz) % 8) * 2 + c) * 4 + j]]
 
     ZORDER = (4, 3, 5, 2, 6, 1, 7, 0)
     ex = {dz: message(xs.at[dz], rx.at[dz], mate) for dz in ZORDER}
-    for dz in ZORDER:
-        for j in range(4):
-            xs[dz, j] = part(dz, 1 - core, j).astype(BF16)
-        ex[dz].start()
 
     up_z = {}
     dn_z = {}
@@ -398,9 +372,42 @@
     U = Scatter(pa, ra1, ra2, ra3, ra4, grad_up, (yp, ym), (xp, xm))
     D = Scatter(pb, rb1, rb2, rb3, rb4, grad_down, (xp, xm), (yp, ym))
 
+    def activate(c, _):
+        act, slope = gelu_parts(pu[tbl[LAST_UP, c]])
+        slope_v[c] = slope
+        ht_v[c] = act.T.astype(BF16)
+        return 0
+
+    def back(c, _):
+        dpre = pd[tbl[LAST_DN, c]] * slope_v[c]
+        dp_v[c] = dpre.astype(BF16)
+        dpt_v[c] = dpre.T.astype(BF16)
+        return 0
+
+    lax.fori_loop(0, 16, activate, 0)
+    for b in (2, 1, 3, 0):
+        D.far(b)
+    lax.fori_loop(0, 16, back, 0)
     for b in (2, 1, 3, 0):
         U.far(b)
-        D.far(b)
+
+    def take_in(n, _):
+        d = []
+        for i in range(4):
+            s = n * 4 + i
+            d.append(dot_nt(dp_v[tbl[UP_COL, s]], ga[n, i]))
+        for i in range(4):
+            s = n * 4 + i
+            pu[s] = d[i] + pu[tbl[PREV_ROW, s]]
+        return 0
+
+    lax.fori_loop(0, 16, take_in, 0)
+
+    for dz in ZORDER:
+        for j in range(4):
+            xs[dz, j] = part(dz, 1 - core, j).astype(BF16)
+        ex[dz].start()
+
     ring(4)
     for b in (2, 1):
         for a in (1, 3):
@@ -432,6 +439,19 @@
     assert count[0] <= 128
 
 
+def hand_over(*refs):
+    src, dst, held, sem = refs[0:3], refs[3:6], refs[6:9], refs[9]
+    take = [pltpu.make_async_copy(src[i], held[i], sem.at[i]) for i in range(3)]
+    give = [pltpu.make_async_copy(held[i], dst[i], sem.at[3 + i]) for i in range(3)]
+    for copy in take:
+        copy.start()
+    for first, second in zip(take, give):
+        first.wait()
+        second.start()
+    for copy in give:
+        copy.wait()
+
+
 def on_device(inputs, cotangent, up_tiles, up_rows, up_cols, down_tiles, down_rows, down_cols):
     tok = inputs.shape[0]
     width = inputs.shape[1]
@@ -441,13 +461,14 @@
     tiles = lambda *n: pltpu.VMEM((*n, TILE, TILE), BF16)
     blocks = lambda *n: pltpu.VMEM((*n, tok, TILE), BF16)
     scatter_bufs = [tiles(2, 4, 2), tiles(2, 4, 4), tiles(2, 2), tiles(2, 4)]
-    return pl.pallas_call(
+    outs = (
+        jax.ShapeDtypeStruct((tok, 4 * TILE), BF16),
+        jax.ShapeDtypeStruct((1, 4, TILE, TILE), BF16),
+        jax.ShapeDtypeStruct((1, 4, TILE, TILE), BF16),
+    )
+    results = pl.pallas_call(
         kernel,
-        out_shape=(
-            jax.ShapeDtypeStruct((tok, 4 * TILE), BF16),
-            jax.ShapeDtypeStruct((1, 4, TILE, TILE), BF16),
-            jax.ShapeDtypeStruct((1, 4, TILE, TILE), BF16),
-        ),
+        out_shape=outs,
         in_specs=[hbm, hbm, hbm, hbm, smem, smem, smem, smem],
         out_specs=(vmem, vmem, vmem),
         scratch_shapes=[
@@ -460,7 +481,7 @@
             pltpu.SMEM((16, TILE), jnp.int32),
             pltpu.VMEM((SLOTS + 1, tok, TILE), F32),
             pltpu.VMEM((SLOTS + 1, tok, TILE), F32),
-            pltpu.VMEM((8, TILE), F32),
+            pltpu.VMEM((16, tok, TILE), F32),
             blocks(16),
             pltpu.VMEM((16, TILE, tok), BF16),
             pltpu.VMEM((16, TILE, tok), BF16),
@@ -480,6 +501,17 @@
             collective_id=0, has_side_effects=True, vmem_limit_bytes=60 * 1024 * 1024
         ),
     )(inputs, cotangent, up_tiles, down_tiles, up_rows, up_cols, down_rows, down_cols)
+    return pl.pallas_call(
+        hand_over,
+        out_shape=outs,
+        in_specs=[hbm] * 3,
+        out_specs=(hbm,) * 3,
+        scratch_shapes=[
+            *(pltpu.VMEM(out.shape, out.dtype) for out in outs),
+            pltpu.SemaphoreType.DMA((6,)),
+        ],
+        compiler_params=pltpu.CompilerParams(vmem_limit_bytes=63 * 1024 * 1024),
+    )(*results)
 
 
 def solution(mesh):

time: 74.2 us -> 73.5 us (level); the launches traced: 74 us -> 72.2 us
  local copies, waits for them, and re-layouts: 4.75 us -> 0 us
  Pallas kernels: 68.6 us -> 71.6 us
    unnamed x3 -> x0, local copies, waits for them, and re-layouts: 4.75 us -> none
    pallas_call x1 -> x2, Pallas kernels: 68.6 us -> 71.6 us  [the longest x1 69.8 us: on_device(): pl.pallas_call(kernel, out_shape=outs, in_specs=[hbm, hbm, hbm, hbm, smem...]
where the time goes in v3:
time: 73.5 us; the launch traced here: 72.2 us
  Pallas kernels  71.6 us (97%)
    pallas_call x1, Pallas kernels, on_device(): pl.pallas_call(kernel, out_shape=outs, in_specs=[hbm, hbm, hbm, hbm, smem...  69.8 us
    pallas_call x1, Pallas kernels, on_device(): pl.pallas_call(hand_over, out_shape=outs, in_specs=[hbm] * 3, out_specs=(...  1.77 us

profile of v3, /device:TPU:6, one launch (start us, length us, event | category | flops | bytes accessed | tf_op | source)
XLA Modules:
  0.0 72.2 jit_solution(10371176782286276817)
XLA Ops:
  0.6 69.8 %shard_map.103 = (bf16[192,512]{1,0:T(8,128)(2,1)}, bf16[1,4,128,128]{3,2,1,0:T(8,128)(2,1)}, bf16[1,4,128,128]{3,2,1,0:T(8,128)(2,1)}) custom-call(bf16[192,8192]{1,0:T(8,128)(2,1)} %x_hbm.1, bf16[192,8192]{1,0:T(8,128)(2,1)} %dy_hbm.1, bf16[1,4,128,128]{3,2,1,0:T(8,128)(2,1)} %up_hbm.1, bf16[1,4,128,128]{3,2,1,0:T(8,128)(2,1)} %down_hbm.1, s32[1,4]{1,0:T(1,128)} %ur.1, ...), custom_call_target="tpu_custom_call" | custom-call | tf_op jit(solution)/shard_map/pallas_call | solution.py:469
  70.4 1.8 %shard_map.104 = (bf16[192,512]{1,0:T(8,128)(2,1)}, bf16[1,4,128,128]{3,2,1,0:T(8,128)(2,1)}, bf16[1,4,128,128]{3,2,1,0:T(8,128)(2,1)}) custom-call(bf16[192,512]{1,0:T(8,128)(2,1)} %get-tuple-element.6.refs_0_, bf16[1,4,128,128]{3,2,1,0:T(8,128)(2,1)} %get-tuple-element.7.refs_1_, bf16[1,4,128,128]{3,2,1,0:T(8,128)(2,1)} %get-tuple-element.8.refs_2_), custom_call_target="tpu_custom_call" | custom-call | tf_op jit(solution)/shard_map/pallas_call | solution.py:504

commit v4 on v1

--- a/solution.py
+++ b/solution.py
@@ -432,6 +432,19 @@
     assert count[0] <= 128
 
 
+def hand_over(*refs):
+    src, dst, held, sem = refs[0:3], refs[3:6], refs[6:9], refs[9]
+    take = [pltpu.make_async_copy(src[i], held[i], sem.at[i]) for i in range(3)]
+    give = [pltpu.make_async_copy(held[i], dst[i], sem.at[3 + i]) for i in range(3)]
+    for copy in take:
+        copy.start()
+    for first, second in zip(take, give):
+        first.wait()
+        second.start()
+    for copy in give:
+        copy.wait()
+
+
 def on_device(inputs, cotangent, up_tiles, up_rows, up_cols, down_tiles, down_rows, down_cols):
     tok = inputs.shape[0]
     width = inputs.shape[1]
@@ -441,13 +454,14 @@
     tiles = lambda *n: pltpu.VMEM((*n, TILE, TILE), BF16)
     blocks = lambda *n: pltpu.VMEM((*n, tok, TILE), BF16)
     scatter_bufs = [tiles(2, 4, 2), tiles(2, 4, 4), tiles(2, 2), tiles(2, 4)]
-    return pl.pallas_call(
+    outs = (
+        jax.ShapeDtypeStruct((tok, 4 * TILE), BF16),
+        jax.ShapeDtypeStruct((1, 4, TILE, TILE), BF16),
+        jax.ShapeDtypeStruct((1, 4, TILE, TILE), BF16),
+    )
+    results = pl.pallas_call(
         kernel,
-        out_shape=(
-            jax.ShapeDtypeStruct((tok, 4 * TILE), BF16),
-            jax.ShapeDtypeStruct((1, 4, TILE, TILE), BF16),
-            jax.ShapeDtypeStruct((1, 4, TILE, TILE), BF16),
-        ),
+        out_shape=outs,
         in_specs=[hbm, hbm, hbm, hbm, smem, smem, smem, smem],
         out_specs=(vmem, vmem, vmem),
         scratch_shapes=[
@@ -480,6 +494,17 @@
             collective_id=0, has_side_effects=True, vmem_limit_bytes=60 * 1024 * 1024
         ),
     )(inputs, cotangent, up_tiles, down_tiles, up_rows, up_cols, down_rows, down_cols)
+    return pl.pallas_call(
+        hand_over,
+        out_shape=outs,
+        in_specs=[hbm] * 3,
+        out_specs=(hbm,) * 3,
+        scratch_shapes=[
+            *(pltpu.VMEM(out.shape, out.dtype) for out in outs),
+            pltpu.SemaphoreType.DMA((6,)),
+        ],
+        compiler_params=pltpu.CompilerParams(vmem_limit_bytes=63 * 1024 * 1024),
+    )(*results)
 
 
 def solution(mesh):

time: 74.2 us -> 71.2 us (0.960)
  local copies, waits for them, and re-layouts: 4.75 us -> 0 us
  Pallas kernels: 68.6 us -> 70.4 us
    unnamed x3 -> x0, local copies, waits for them, and re-layouts: 4.75 us -> none
    pallas_call x1 -> x2, Pallas kernels: 68.6 us -> 70.4 us  [the longest x1 68.6 us: on_device(): pl.pallas_call(kernel, out_shape=outs, in_specs=[hbm, hbm, hbm, hbm, smem...]
where the time goes in v4:
time: 71.2 us; the launch traced here: 71 us
  Pallas kernels  70.4 us (99%)
    pallas_call x1, Pallas kernels, on_device(): pl.pallas_call(kernel, out_shape=outs, in_specs=[hbm, hbm, hbm, hbm, smem...  68.6 us
    pallas_call x1, Pallas kernels, on_device(): pl.pallas_call(hand_over, out_shape=outs, in_specs=[hbm] * 3, out_specs=(...  1.77 us

profile of v4, /device:TPU:6, one launch (start us, length us, event | category | flops | bytes accessed | tf_op | source)
XLA Modules:
  0.0 71.0 jit_solution(15932080291349805433)
XLA Ops:
  0.6 68.6 %shard_map.103 = (bf16[192,512]{1,0:T(8,128)(2,1)}, bf16[1,4,128,128]{3,2,1,0:T(8,128)(2,1)}, bf16[1,4,128,128]{3,2,1,0:T(8,128)(2,1)}) custom-call(bf16[192,8192]{1,0:T(8,128)(2,1)} %x_hbm.1, bf16[192,8192]{1,0:T(8,128)(2,1)} %dy_hbm.1, bf16[1,4,128,128]{3,2,1,0:T(8,128)(2,1)} %up_hbm.1, bf16[1,4,128,128]{3,2,1,0:T(8,128)(2,1)} %down_hbm.1, s32[1,4]{1,0:T(1,128)} %ur.1, ...), custom_call_target="tpu_custom_call" | custom-call | tf_op jit(solution)/shard_map/pallas_call | solution.py:462
  69.3 1.8 %shard_map.104 = (bf16[192,512]{1,0:T(8,128)(2,1)}, bf16[1,4,128,128]{3,2,1,0:T(8,128)(2,1)}, bf16[1,4,128,128]{3,2,1,0:T(8,128)(2,1)}) custom-call(bf16[192,512]{1,0:T(8,128)(2,1)} %get-tuple-element.6.refs_0_, bf16[1,4,128,128]{3,2,1,0:T(8,128)(2,1)} %get-tuple-element.7.refs_1_, bf16[1,4,128,128]{3,2,1,0:T(8,128)(2,1)} %get-tuple-element.8.refs_2_), custom_call_target="tpu_custom_call" | custom-call | tf_op jit(solution)/shard_map/pallas_call | solution.py:497
